TPU v7x, 512 devices: a whole 4x8x8 slice. The times are simulated.
512 devices in a mesh: st: 8 (over x, core), fsdp: 64 (over z, y).
Axes of the slice: x: 4, y: 8, z: 8, core: 2. Of those that a mesh axis runs over, the one named last changes fastest.
Arguments:
- normed: bfloat16 [64, 512, 3072], P('fsdp')
- qkv_weight: bfloat16 [3072, 32, 384], P('fsdp', 'st'), may hold values from -0.109375 to 0.109375
- out_weight: bfloat16 [3072, 4096], P('fsdp', 'st'), may hold values from -0.09375 to 0.09375
- segment_ids: int32 [64], replicated, may hold values from 0 to 15, never falling along the last dimension, each value on 1 to 8 neighbouring positions
Outputs:
- attended: bfloat16 [64, 512, 3072], P('fsdp', 'st')
Inputs may be any that keep to these rules, and one draw needn't show every extreme that they name: `segment_ids`: segment ids never fall from one frame to the next; each clip covers 1 to 8 consecutive frames, and one covers exactly 8.
All inputs are finite; a program needn't handle non-finite values.
Results may differ from a plain program's by a relative error of at most 0.017.
Values may be sent and summed in bfloat16 or wider, within the bound.
A program may use at most 64 MiB of HBM per device.

v0:
```python
import math

import jax
import jax.numpy as jnp
from jax import lax
from jax.sharding import PartitionSpec as P

HEAD = 128
HS_DEV = 2


def softmax_rows(scores):
    top = jnp.max(scores, axis=-1, keepdims=True)
    expo = jnp.exp(scores - top)
    return expo / jnp.sum(expo, axis=-1, keepdims=True)


def shards(normed, qkv_weight, out_weight, segment_ids):
    patches = normed.shape[1]
    width = normed.shape[2]
    group = qkv_weight.shape[1]
    scale = 1.0 / math.sqrt(HEAD)
    frame_rows = normed.reshape(patches, width)
    projected = jnp.einsum(
        "pd,dhc->phc",
        frame_rows,
        lax.all_gather(qkv_weight, "fsdp", axis=0, tiled=True),
        preferred_element_type=jnp.float32,
    )
    out_full = lax.all_gather(out_weight, "fsdp", axis=0, tiled=True)
    packed = projected.astype(jnp.bfloat16)
    spatial = packed[:, :HS_DEV]
    scores = (
        jnp.einsum(
            "qhc,khc->hqk",
            spatial[..., :HEAD],
            spatial[..., HEAD : 2 * HEAD],
            preferred_element_type=jnp.float32,
        )
        * scale
    )
    weights = softmax_rows(scores).astype(jnp.bfloat16)
    spatial_out = jnp.einsum(
        "hqk,khc->qhc", weights, spatial[..., 2 * HEAD :], preferred_element_type=jnp.float32
    ).astype(jnp.bfloat16)
    temporal_in = packed[:, HS_DEV:].reshape(1, patches, group - HS_DEV, 3 * HEAD)
    block = lax.all_to_all(temporal_in, "fsdp", split_axis=1, concat_axis=0, tiled=True)
    query = block[..., :HEAD]
    keys = block[..., HEAD : 2 * HEAD]
    values = block[..., 2 * HEAD :]
    all_scores = (
        jnp.einsum("tphc,uphc->phtu", query, keys, preferred_element_type=jnp.float32) * scale
    )
    same = segment_ids[:, None] == segment_ids[None, :]
    all_scores = jnp.where(same, all_scores, jnp.float32(-1e30))
    all_weights = softmax_rows(all_scores).astype(jnp.bfloat16)
    result = jnp.einsum("phtu,uphc->tphc", all_weights, values, preferred_element_type=jnp.float32)
    temporal_out = lax.all_to_all(
        result.astype(jnp.bfloat16), "fsdp", split_axis=0, concat_axis=1, tiled=True
    )
    heads_out = jnp.concatenate(
        [spatial_out, temporal_out.reshape(patches, group - HS_DEV, HEAD)], axis=1
    )
    heads_out = heads_out.reshape(patches, group * HEAD)
    summed = lax.psum_scatter(
        lax.dot_general(
            heads_out, out_full, (((1,), (1,)), ((), ())), preferred_element_type=jnp.float32
        ).astype(jnp.bfloat16),
        "st",
        scatter_dimension=0,
        tiled=True,
    ).astype(jnp.float32)
    return summed.astype(jnp.bfloat16).reshape(1, summed.shape[0], width)


def solution(mesh):
    return jax.shard_map(
        shards,
        mesh=mesh,
        in_specs=(P("fsdp", None, None), P("fsdp", "st", None), P("fsdp", "st"), P()),
        out_specs=P("fsdp", "st", None),
        check_vma=False,
    )
```

profile of v0, /device:TPU:1, one launch (start us, length us, event | category | flops | bytes accessed | tf_op | source)
XLA Modules:
  0.0 263.6 jit_solution(5956684058588850839)
XLA Ops:
  6.5 1.7 copy.30
  8.4 0.7 all-gather.5.cloned.1.call-update
  9.1 111.4 %all-gather.3.cloned.1.call-done = bf16[3072,4,384]{2,0,1:T(8,128)(2,1)} async-done(((bf16[48,4,384]{2,0,1:T(8,128)(2,1)}), bf16[3072,4,384]{2,0,1:T(8,128)(2,1)}) %all-gather.3.cloned.1.call-update) | async-done | bytes 9437200 | tf_op jit(solution)/shard_map/all_gather | solution.py:27
  120.5 7.8 %fusion.5 = bf16[512,4,384]{2,0,1:T(8,128)(2,1)S(1)} fusion(bf16[3072,4,384]{2,0,1:T(8,128)(2,1)} %all-gather.3.cloned.1.call-done, bf16[1,512,3072]{2,1,0:T(8,128)(2,1)S(1)} %copy-done), kind=kOutput, calls=%fused_computation.9 | convolution fusion | flops 4832624640 | bytes 14155776 | tf_op jit(solution)/shard_map/pd,dhc->phc/dot_general | solution.py:24
  128.3 1.1 copy-done.1
  129.5 1.7 copy.33
  131.2 10.0 %all-to-all-start = ((bf16[1,512,2,384]{3,2,0,1:T(2,128)(2,1)}), bf16[1,512,2,384]{3,2,0,1:T(2,128)(2,1)}, u32[]{:S(2)}, u32[]{:S(2)}) async-start(bf16[1,512,2,384]{3,2,0,1:T(2,128)(2,1)} %copy.33), calls=%async_computation | async-start | bytes 1572864 | tf_op jit(solution)/shard_map/all_to_all | solution.py:47
  141.3 22.5 %all-to-all-done = bf16[1,512,2,384]{3,2,0,1:T(2,128)(2,1)} async-done(((bf16[1,512,2,384]{3,2,0,1:T(2,128)(2,1)}), bf16[1,512,2,384]{3,2,0,1:T(2,128)(2,1)}, u32[]{:S(2)}, u32[]{:S(2)}) %all-to-all-start) | async-done | bytes 786464 | tf_op jit(solution)/shard_map/all_to_all | solution.py:47
  163.9 1.2 copy.57
  165.1 0.8 fusion.51
  165.9 0.3 fusion.10
  166.2 0.1 fusion.52
  166.4 0.7 copy-done.3
  167.0 1.6 fusion.11
  168.6 1.0 copy.39
  169.6 8.0 %all-to-all-start.1 = ((bf16[64,8,2,128]{3,2,1,0:T(2,128)(2,1)}), bf16[64,8,2,128]{3,2,1,0:T(2,128)(2,1)S(1)}, u32[]{:S(2)}, u32[]{:S(2)}) async-start(bf16[64,8,2,128]{3,2,1,0:T(2,128)(2,1)} %copy.39), calls=%async_computation.1 | async-start | bytes 524288 | tf_op jit(solution)/shard_map/all_to_all | solution.py:58
  177.7 1.8 fusion.53
  179.5 2.9 %fusion.12 = bf16[512,2,128]{0,2,1:T(8,128)(2,1)} fusion(f32[2,512]{1,0:T(2,128)S(1)} %fusion.53, bf16[512,4,384]{2,0,1:T(8,128)(2,1)} %copy-done.1), kind=kOutput, calls=%fused_computation.17 | convolution fusion | flops 270665216 | bytes 1052672 | tf_op jit(solution)/shard_map/hqk,khc->qhc/dot_general | solution.py:43
  182.4 7.8 %all-to-all-done.1 = bf16[64,8,2,128]{3,2,1,0:T(2,128)(2,1)S(1)} async-done(((bf16[64,8,2,128]{3,2,1,0:T(2,128)(2,1)}), bf16[64,8,2,128]{3,2,1,0:T(2,128)(2,1)S(1)}, u32[]{:S(2)}, u32[]{:S(2)}) %all-to-all-start.1) | async-done | bytes 262176 | tf_op jit(solution)/shard_map/all_to_all | solution.py:58
  190.2 0.9 copy.41
  191.1 1.9 pad_maximum_fusion
  192.9 19.2 %all-gather.5.cloned.1.call-done = bf16[3072,512]{1,0:T(8,128)(2,1)} async-done(((bf16[48,512]{1,0:T(8,128)(2,1)}), bf16[3072,512]{1,0:T(8,128)(2,1)}) %all-gather.5.cloned.1.call-update) | async-done | bytes 3145744 | tf_op jit(solution)/shard_map/all_gather | solution.py:30
  212.1 5.6 %convolution_convert_fusion = bf16[512,3072]{1,0:T(8,128)(2,1)} fusion(bf16[512,512]{0,1:T(8,128)(2,1)} %bitcast.25, bf16[3072,512]{1,0:T(8,128)(2,1)} %all-gather.5.cloned.1.call-done), kind=kOutput, calls=%fused_computation.2 | convolution fusion | flops 1612185600 | bytes 6815744 | tf_op jit(solution)/shard_map/dot_general | solution.py:66
  217.7 39.4 %reduce-scatter.2.cloned.1.call-done = bf16[64,3072]{1,0:T(8,128)(2,1)} async-done(((bf16[512,3072]{1,0:T(8,128)(2,1)}), bf16[64,3072]{1,0:T(8,128)(2,1)}) %reduce-scatter.2.cloned.1.call-update) | async-done | bytes 393232 | tf_op jit(solution)/shard_map/reduce_scatter | solution.py:65
  (13 shorter events, 0.3 us)
Async XLA Ops:
  6.5 113.9 %copy-start = (bf16[1,512,3072]{2,1,0:T(8,128)(2,1)S(1)}, bf16[1,512,3072]{2,1,0:T(8,128)(2,1)}, u32[]{:S(2)}) copy-start(bf16[1,512,3072]{2,1,0:T(8,128)(2,1)} %param.4) | copy-start | bytes 9437188
  6.5 113.9 %all-gather.3.cloned.1.call-start = ((), (), s32[]{:S(2)}) async-start(), calls=%async_computation.3 | async-start | bytes 9584640 | tf_op jit(solution)/shard_map/all_gather | solution.py:27
  8.3 203.8 %all-gather.5.cloned.1.call-start = ((), (), s32[]{:S(2)}) async-start(), calls=%async_computation.4 | async-start | bytes 3194880 | tf_op jit(solution)/shard_map/all_gather | solution.py:30
  128.2 1.2 copy-start.1
  129.4 11.8 %copy-start.2 = (s32[64]{0:T(128)S(1)}, s32[64]{0:T(128)}, u32[]{:S(2)}) copy-start(s32[64]{0:T(128)} %param.7) | copy-start | bytes 772
  131.2 32.7 %all-to-all-start = ((bf16[1,512,2,384]{3,2,0,1:T(2,128)(2,1)}), bf16[1,512,2,384]{3,2,0,1:T(2,128)(2,1)}, u32[]{:S(2)}, u32[]{:S(2)}) async-start(bf16[1,512,2,384]{3,2,0,1:T(2,128)(2,1)} %copy.33), calls=%async_computation | async-start | bytes 1572864 | tf_op jit(solution)/shard_map/all_to_all | solution.py:47
  166.2 0.8 copy-start.3
  169.6 20.6 %all-to-all-start.1 = ((bf16[64,8,2,128]{3,2,1,0:T(2,128)(2,1)}), bf16[64,8,2,128]{3,2,1,0:T(2,128)(2,1)S(1)}, u32[]{:S(2)}, u32[]{:S(2)}) async-start(bf16[64,8,2,128]{3,2,1,0:T(2,128)(2,1)} %copy.39), calls=%async_computation.1 | async-start | bytes 524288 | tf_op jit(solution)/shard_map/all_to_all | solution.py:58
  177.6 79.5 %reduce-scatter.2.cloned.1.call-start = ((), (), s32[]{:S(2)}) async-start(), calls=%async_computation.5 | async-start | bytes 3538944 | tf_op jit(solution)/shard_map/reduce_scatter | solution.py:65
Sparse Core Ops, SparseCore 0:
  10.4 110.0 all-gather.2
  123.5 88.5 all-gather.4
  217.8 39.2 reduce-scatter.1
where the time goes:
time: 265 us; the launch traced here: 264 us
  waiting for transfers between devices  201 us (76%)
  matrix products  20 us (8%)
  starting transfers between devices  18.1 us (7%)
  between operations  13.2 us (5%)
  local copies, waits for them, and re-layouts  9.24 us (3%)
    all_gather x1, waiting for transfers between devices, shards(): lax.all_gather(qkv_weight, 'fsdp', axis=0, tiled=True)  111 us
    reduce_scatter x1, waiting for transfers between devices, shards(): lax.psum_scatter(lax.dot_general(heads_out, out_full, (((1,), (1,)), ((),...  39.4 us
    all_to_all x1, waiting for transfers between devices, shards(): lax.all_to_all(temporal_in, 'fsdp', split_axis=1, concat_axis=0, tiled=True)  22.5 us
    all_gather x1, waiting for transfers between devices, shards(): out_full = lax.all_gather(out_weight, 'fsdp', axis=0, tiled=True)  19.2 us
    all_to_all x1, starting transfers between devices, shards(): lax.all_to_all(temporal_in, 'fsdp', split_axis=1, concat_axis=0, tiled=True)  10 us
    all_to_all x1, starting transfers between devices, shards(): lax.all_to_all(result.astype(jnp.bfloat16), 'fsdp', split_axis=0, concat_...  8 us
    dot_general x1, matrix products, shards(): jnp.einsum('pd,dhc->phc', frame_rows, lax.all_gather(qkv_weight, 'fsdp',...  7.76 us
    all_to_all x1, waiting for transfers between devices, shards(): lax.all_to_all(result.astype(jnp.bfloat16), 'fsdp', split_axis=0, concat_...  7.75 us
  transfers between devices with their start and end apart: 5, of which 5 were waited for; matrix products, arithmetic and copies ran while one was open for 8% of the time, Pallas kernels for 0%

commit v1 on v0

v1 whole, which is shorter than its diff:
```python
import functools
import math

import jax
import jax.numpy as jnp
from jax import lax
from jax.experimental import pallas as pl
from jax.experimental.pallas import tpu as pltpu
from jax.sharding import PartitionSpec as P

HEAD = 128
MESH = pl.DeviceIdType.MESH
NZ = NY = 8
NX = 4
PIECE = 48
QKV = 3 * HEAD
SLAB = 384
PATCHES = 512
WIDTH = 3072
UP = ((-1, 0), (-1, 1), (-2, 0), (-2, 1), (-3, 0), (-3, 1), (-4, 0))
DOWN = ((1, 1), (1, 0), (2, 1), (2, 0), (3, 1), (3, 0), (4, 1))
F32 = jnp.float32
BF16 = jnp.bfloat16


def nt_dot(a, b):
    return lax.dot_general(a, b, (((1,), (1,)), ((), ())), preferred_element_type=F32)


def nn_dot(a, b):
    return lax.dot_general(a, b, (((1,), (0,)), ((), ())), preferred_element_type=F32)


def softmax_rows(scores):
    top = jnp.max(scores, axis=-1, keepdims=True)
    expo = jnp.exp(scores - top)
    return expo * (1.0 / jnp.sum(expo, axis=-1, keepdims=True))


def kernel(
    seg_ref, x_ref, x4_ref, wq_ref, wo_ref, out_ref,
    xs, w, wo, r1, a, xt, acc, qt, qs, ot, b1, b2, ho, p, c, d, f, idc, idr,
    gs, gr, ns, nr, hs, hr, ts, tr, vs, vr, loc,
):
    st, fs = lax.axis_index("st"), lax.axis_index("fsdp")
    x, core = st // 2, st % 2
    z, y = fs // NY, fs % NY
    scale = 1.0 / math.sqrt(HEAD)
    sent = []

    def dev_y(k):
        return (st, z * NY + (y + k) % NY)

    def dev_z(k):
        return (st, ((z + k) % NZ) * NY + y)

    def dev_x(k):
        return (((x + k) % NX) * 2 + core, fs)

    sibling = (x * 2 + 1 - core, fs)

    def remote(src, dst, ssem, rsem, dev):
        return pltpu.make_async_remote_copy(
            src_ref=src, dst_ref=dst, send_sem=ssem, recv_sem=rsem, device_id=dev, device_id_type=MESH
        )

    def send(*args):
        copy = remote(*args)
        copy.start()
        sent.append(copy)

    barrier = pltpu.get_barrier_semaphore()
    for k in range(1, 8):
        pl.semaphore_signal(barrier, inc=1, device_id=dev_y(k), device_id_type=MESH)
        pl.semaphore_signal(barrier, inc=1, device_id=dev_z(k), device_id_type=MESH)
    for k in range(1, 4):
        pl.semaphore_signal(barrier, inc=1, device_id=dev_x(k), device_id_type=MESH)
    pl.semaphore_signal(barrier, inc=1, device_id=sibling, device_id_type=MESH)
    pl.semaphore_wait(barrier, 18)

    class Stream:
        def __init__(self, number, y_first, flip, own, view):
            self.n, self.y_first, self.flip, self.own, self.view = number, y_first, flip, own, view
            self.ac, self.bc = (y, z) if y_first else (z, y)
            self.da, self.db = (dev_y, dev_z) if y_first else (dev_z, dev_y)

        def piece(self, at):
            return self.view(self.bc, at) if self.y_first else self.view(at, self.bc)

        def slab(self, bt, sub):
            four = pl.ds(4 * sub, 4)
            return self.view(bt, four) if self.y_first else self.view(four, bt)

        def sems(self, i):
            return gs.at[self.n, i], gr.at[self.n, i]

        def first_own(self):
            right = 1 if not self.flip else -1
            send(self.own, self.piece(self.ac), *self.sems(0), self.da(right))
            send(self.own, self.piece(self.ac), *self.sems(4), self.da(-right))

        def first(self, k):
            right = 1 if not self.flip else -1
            for way, base, last in ((right, 0, 4), (-right, 4, 3)):
                if k <= last:
                    got = self.piece((self.ac - way * k) % 8)
                    remote(got, got, *self.sems(base + k - 1), self.da(-way)).wait_recv()
                    if k < last:
                        send(got, got, *self.sems(base + k), self.da(way))

        def second_own(self):
            for sub in (0, 1):
                for way, base, chain in ((1, 7, UP), (-1, 14, DOWN)):
                    blk = self.slab(self.bc, chain[sub][1])
                    send(blk, blk, *self.sems(base + sub), self.db(way))

        def second(self, i):
            for way, base, chain in ((1, 7, UP), (-1, 14, DOWN)):
                off, sub = chain[i]
                got = self.slab((self.bc + off) % 8, sub)
                remote(got, got, *self.sems(base + i), self.db(-way)).wait_recv()
                if i <= 4:
                    send(got, got, *self.sems(base + i + 2), self.db(way))

    def head_stream(number, h, y_first, flip):
        return Stream(number, y_first, flip, wq_ref.at[h], lambda zi, yi: w.at[h, zi, yi])

    s0 = head_stream(2, 0, True, True)
    s1 = head_stream(3, 1, False, True)
    t0 = head_stream(0, 2, True, False)
    t1 = head_stream(1, 3, False, False)
    o0 = Stream(4, True, False, wo_ref.at[pl.ds(0, 32)], lambda zi, yi: wo.at[zi, yi, pl.ds(0, 32)])
    o1 = Stream(5, False, False, wo_ref.at[pl.ds(32, 16)], lambda zi, yi: wo.at[zi, yi, pl.ds(32, 16)])

    cols = pl.ds(pl.multiple_of(st * SLAB, SLAB), SLAB)
    for k in range(1, 8):
        yy = (y + k) % NY
        send(x4_ref.at[:, yy, :, cols], r1.at[y], ns.at[k - 1], nr.at[k - 1], dev_y(k))
    for s in (t0, t1, s0, s1, o1, o0):
        s.first_own()
    locals_ = [
        pltpu.make_async_copy(x4_ref.at[:, y, :, cols], r1.at[y], loc.at[0]),
        pltpu.make_async_copy(wo_ref, wo.at[z, y], loc.at[1]),
    ]
    for h in range(4):
        locals_.append(pltpu.make_async_copy(wq_ref.at[h], w.at[h, z, y], loc.at[2 + h]))
    locals_.append(pltpu.make_async_copy(x_ref, xs, loc.at[6]))
    for cp in locals_:
        cp.start()

    sub8 = lax.broadcasted_iota(jnp.int32, (8, HEAD), 0)
    lane = lax.broadcasted_iota(jnp.int32, (8, PATCHES), 1)
    row = jnp.zeros((8, PATCHES), jnp.int32)
    for t in range(64):
        sid = seg_ref[t]
        idc[t * 8 : (t + 1) * 8, :] = sub8 + sid * 8
        row = jnp.where(lane // 8 == t, sid * 8, row)
    idr[...] = row + lane % 8

    for cp in locals_[:6]:
        cp.wait()

    for k in range(1, 5):
        t0.first(k)
        t1.first(k)
    t0.second_own()
    t1.second_own()
    for k in range(1, 8):
        got = r1.at[(y - k) % NY]
        remote(got, got, ns.at[k - 1], nr.at[k - 1], dev_y(-k)).wait_recv()
    for k in range(1, 8):
        zz = (z + k) % NZ
        send(r1.at[:, zz], a.at[st, z], ns.at[6 + k], nr.at[6 + k], dev_z(k))
    own_tile = pltpu.make_async_copy(r1.at[:, z], a.at[st, z], loc.at[7])
    own_tile.start()
    for k in range(1, 5):
        for s in (s0, s1, o1, o0):
            s.first(k)
    own_tile.wait()
    t0.second(0)
    t1.second(0)
    for k in range(1, 8):
        got = a.at[st, (z - k) % NZ]
        remote(got, got, ns.at[6 + k], nr.at[6 + k], dev_z(-k)).wait_recv()
    sl_m, sl_p, sl_2 = (((x + k) % NX) * 2 + core for k in (3, 1, 2))
    send(a.at[st], a.at[st], ns.at[14], nr.at[14], dev_x(1))
    send(a.at[st], a.at[st], ns.at[15], nr.at[15], dev_x(-1))
    send(a.at[st], a.at[st], ns.at[18], nr.at[18], sibling)
    t0.second(1)
    t1.second(1)

    def assemble(sl):
        def body(i, _):
            v = a[sl, i].astype(F32).reshape(64, SLAB)
            xt[sl, pl.ds(pl.multiple_of(i * 64, 64), 64), :] = v.astype(BF16)
            return 0

        lax.fori_loop(0, 8, body, 0)

    assemble(st)
    t0.second(2)
    t1.second(2)
    lo, hi = pl.ds(0, 4), pl.ds(4, 4)
    remote(a.at[sl_m], a.at[sl_m], ns.at[14], nr.at[14], dev_x(-1)).wait_recv()
    send(a.at[sl_m, lo], a.at[sl_m, lo], ns.at[16], nr.at[16], dev_x(1))
    send(a.at[sl_m], a.at[sl_m], ns.at[19], nr.at[19], sibling)
    remote(a.at[sl_p], a.at[sl_p], ns.at[15], nr.at[15], dev_x(1)).wait_recv()
    send(a.at[sl_p, hi], a.at[sl_p, hi], ns.at[17], nr.at[17], dev_x(-1))
    send(a.at[sl_p], a.at[sl_p], ns.at[20], nr.at[20], sibling)
    assemble(sl_m)
    assemble(sl_p)
    t0.second(3)
    t1.second(3)
    remote(a.at[sl_2, lo], a.at[sl_2, lo], ns.at[16], nr.at[16], dev_x(-1)).wait_recv()
    remote(a.at[sl_2, hi], a.at[sl_2, hi], ns.at[17], nr.at[17], dev_x(1)).wait_recv()
    send(a.at[sl_2], a.at[sl_2], ns.at[21], nr.at[21], sibling)
    assemble(sl_2)
    t0.second(4)
    t1.second(4)
    s0.second_own()
    s1.second_own()
    flip = 1 - 2 * core
    for i, sl in enumerate((st, sl_m, sl_p, sl_2)):
        other = sl + flip
        remote(a.at[other], a.at[other], ns.at[18 + i], nr.at[18 + i], sibling).wait_recv()
        assemble(other)
    for i in (5, 6):
        t0.second(i)
        t1.second(i)

    def proj(load, h, dest):
        acc[...] = jnp.zeros_like(acc)

        def body(i, _):
            acc[...] += nn_dot(load(i), w[h, i].reshape(SLAB, QKV))
            return 0

        lax.fori_loop(0, 8, body, 0)
        dest[...] = acc[...].astype(BF16)

    proj(lambda i: xt[i], 2, qt.at[0])
    s0.second(0)
    s1.second(0)
    proj(lambda i: xt[i], 3, qt.at[1])
    s0.second(1)
    s1.second(1)

    for h in (0, 1):
        for b, start in enumerate((0, 64, 192, 256)):
            rows, keys = pl.ds(b * 128, 128), pl.ds(start, 256)
            s = nt_dot(qt[h, rows, 0:HEAD], qt[h, keys, HEAD : 2 * HEAD]) * scale
            same = idc[rows, 0:1] == idr[0:1, keys]
            wt = softmax_rows(jnp.where(same, s, -1e30)).astype(BF16)
            o = nn_dot(wt, qt[h, keys, 2 * HEAD :])
            ot[2 * b : 2 * b + 2, :, :, h * HEAD : (h + 1) * HEAD] = o.reshape(2, 8, 8, HEAD).astype(BF16)
    for k in range(1, 8):
        zz = (z + k) % NZ
        send(ot.at[zz], b1.at[z], ts.at[k - 1], tr.at[k - 1], dev_z(k))
    back = pltpu.make_async_copy(ot.at[z], b1.at[z], loc.at[8])
    back.start()
    s0.second(2)
    s1.second(2)
    back.wait()
    for k in range(1, 8):
        got = b1.at[(z - k) % NZ]
        remote(got, got, ts.at[k - 1], tr.at[k - 1], dev_z(-k)).wait_recv()
    for k in range(1, 8):
        yy = (y + k) % NY
        send(b1.at[:, yy], b2.at[:, y], ts.at[6 + k], tr.at[6 + k], dev_y(k))
    back2 = pltpu.make_async_copy(b1.at[:, y], b2.at[:, y], loc.at[9])
    back2.start()
    s0.second(3)
    s1.second(3)
    s0.second(4)
    s1.second(4)
    o1.second_own()
    o0.second_own()
    for i in (5, 6):
        s0.second(i)
        s1.second(i)
    locals_[6].wait()
    back2.wait()

    def own_rows(i):
        return xs[:, pl.ds(pl.multiple_of(i * SLAB, SLAB), SLAB)]

    def spatial(h):
        def body(i, _):
            rows = pl.ds(pl.multiple_of(i * 128, 128), 128)
            s = nt_dot(qs[h, rows, 0:HEAD], qs[h, :, HEAD : 2 * HEAD]) * scale
            o = nn_dot(softmax_rows(s).astype(BF16), qs[h, :, 2 * HEAD :])
            ho[rows, h * HEAD : (h + 1) * HEAD] = o.astype(BF16)
            return 0

        lax.fori_loop(0, 4, body, 0)

    proj(own_rows, 0, qs.at[0])
    o1.second(0)
    o0.second(0)
    proj(own_rows, 1, qs.at[1])
    o1.second(1)
    o0.second(1)
    spatial(0)
    o1.second(2)
    o0.second(2)
    spatial(1)
    o1.second(3)
    o0.second(3)
    for k in range(1, 8):
        got = b2.at[:, (y - k) % NY]
        remote(got, got, ts.at[6 + k], tr.at[6 + k], dev_y(-k)).wait_recv()
    for i in range(8):
        ho[i * 64 : (i + 1) * 64, 2 * HEAD :] = b2[i].astype(F32).reshape(64, 2 * HEAD).astype(BF16)
    for i in (4, 5, 6):
        o1.second(i)

    order = (0, -1, 1, -2, 2, -3, 3, 4)

    def project(j):
        n = (z + order[j]) % NZ
        o = nt_dot(ho[...], wo[n].reshape(SLAB, 4 * HEAD))
        p[j] = o.astype(BF16).reshape(NX, 2, 64, SLAB)
        send(p.at[j, :, 1 - core], c.at[j], vs.at[j, 0], vr.at[j, 0], sibling)

    def pair(j):
        remote(c.at[j], c.at[j], vs.at[j, 0], vr.at[j, 0], sibling).wait_recv()
        d[j] = (p[j, :, core].astype(F32) + c[j].astype(F32)).astype(BF16)
        for k in (1, 2, 3):
            send(d.at[j, (x + k) % NX], f.at[j, k - 1], vs.at[j, k], vr.at[j, k], dev_x(k))

    def finish(j):
        total = d[j, x].astype(F32)
        for k in (1, 2, 3):
            got = f.at[j, k - 1]
            remote(got, got, vs.at[j, k], vr.at[j, k], dev_x(-k)).wait_recv()
            total = total + f[j, k - 1].astype(F32)
        n = (z + order[j]) % NZ
        out_ref[:, pl.ds(pl.multiple_of(n * SLAB, SLAB), SLAB)] = total.astype(BF16)

    for j in range(5):
        project(j)
        if j >= 1:
            pair(j - 1)
    o0.second(4)
    o0.second(5)
    project(5)
    pair(4)
    project(6)
    pair(5)
    o0.second(6)
    project(7)
    pair(6)
    pair(7)
    for j in range(8):
        finish(j)
    for copy in sent:
        copy.wait_send()


def shards(normed, qkv_weight, out_weight, segment_ids):
    rows = normed.reshape(PATCHES, WIDTH)
    tiles = normed.reshape(NZ, NY, 8, WIDTH)
    heads = jnp.transpose(qkv_weight, (1, 0, 2))
    dma = pltpu.SemaphoreType.DMA
    out = pl.pallas_call(
        kernel,
        out_shape=jax.ShapeDtypeStruct((64, WIDTH), BF16),
        in_specs=[pl.BlockSpec(memory_space=pltpu.SMEM)] + [pl.BlockSpec(memory_space=pl.ANY)] * 4,
        out_specs=pl.BlockSpec(memory_space=pltpu.VMEM),
        scratch_shapes=[
            pltpu.VMEM((PATCHES, WIDTH), BF16),
            pltpu.VMEM((4, NZ, NY, PIECE, QKV), BF16),
            pltpu.VMEM((NZ, NY, PIECE, 4 * HEAD), BF16),
            pltpu.VMEM((NY, NZ, 8, SLAB), BF16),
            pltpu.VMEM((8, NZ, NY, 8, SLAB), BF16),
            pltpu.VMEM((8, PATCHES, SLAB), BF16),
            pltpu.VMEM((PATCHES, QKV), F32),
            pltpu.VMEM((2, PATCHES, QKV), BF16),
            pltpu.VMEM((2, PATCHES, QKV), BF16),
            pltpu.VMEM((NZ, NY, 8, 2 * HEAD), BF16),
            pltpu.VMEM((NZ, NY, 8, 2 * HEAD), BF16),
            pltpu.VMEM((NZ, NY, 8, 2 * HEAD), BF16),
            pltpu.VMEM((PATCHES, 4 * HEAD), BF16),
            pltpu.VMEM((8, NX, 2, 64, SLAB), BF16),
            pltpu.VMEM((8, NX, 64, SLAB), BF16),
            pltpu.VMEM((8, NX, 64, SLAB), BF16),
            pltpu.VMEM((8, 3, 64, SLAB), BF16),
            pltpu.VMEM((PATCHES, HEAD), jnp.int32),
            pltpu.VMEM((8, PATCHES), jnp.int32),
            dma((6, 21)), dma((6, 21)),
            dma((22,)), dma((22,)),
            dma((1,)), dma((1,)),
            dma((14,)), dma((14,)),
            dma((8, 4)), dma((8, 4)),
            dma((10,)),
        ],
        compiler_params=pltpu.CompilerParams(
            collective_id=0, has_side_effects=True, vmem_limit_bytes=58 * 2**20
        ),
        name="whole",
    )(segment_ids, rows, tiles, heads, out_weight)
    return out.reshape(1, 64, WIDTH)


def solution(mesh):
    return jax.shard_map(
        shards,
        mesh=mesh,
        in_specs=(P("fsdp", None, None), P("fsdp", "st", None), P("fsdp", "st"), P()),
        out_specs=P("fsdp", "st", None),
        check_vma=False,
    )
```

time: 265 us -> 155 us (0.58)
  waiting for transfers between devices: 201 us -> 0 us
  Pallas kernels: 0 us -> 152 us
  matrix products: 20 us -> 0 us
  starting transfers between devices: 18.1 us -> 0 us
  between operations: 13.2 us -> 0.01 us
  local copies, waits for them, and re-layouts: 9.24 us -> 3.36 us
    pallas_call x0 -> x1, Pallas kernels: none -> 152 us  [shards(): pl.pallas_call(kernel, out_shape=jax.ShapeDtypeStruct((64, WIDTH), BF16),...]
    all_gather x2 -> x0, waiting for transfers between devices: 131 us -> none  [the longest x1 111 us: shards(): lax.all_gather(qkv_weight, 'fsdp', axis=0, tiled=True)]
    reduce_scatter x1 -> x0, waiting for transfers between devices: 39.4 us -> none  [shards(): lax.psum_scatter(lax.dot_general(heads_out, out_full, (((1,), (1,)), ((),...]
    all_to_all x2 -> x0, waiting for transfers between devices: 30.3 us -> none  [the longest x1 22.5 us: shards(): lax.all_to_all(temporal_in, 'fsdp', split_axis=1, concat_axis=0, tiled=True)]
    dot_general x5 -> x0, matrix products: 18.2 us -> none  [the longest x1 7.76 us: shards(): jnp.einsum('pd,dhc->phc', frame_rows, lax.all_gather(qkv_weight, 'fsdp',...]
    all_to_all x2 -> x0, starting transfers between devices: 18 us -> none  [the longest x1 10 us: shards(): lax.all_to_all(temporal_in, 'fsdp', split_axis=1, concat_axis=0, tiled=True)]
    reshape x3 -> x0, local copies, waits for them, and re-layouts: 2.65 us -> none  [the longest x2 1.78 us: shards(): packed[:, HS_DEV:].reshape(1, patches, group - HS_DEV, 3 * HEAD)]
  transfers between devices with their start and end apart: 5 -> 0, of which waited for: 5 -> 0; matrix products, arithmetic and copies ran while one was open for 8% -> 0% of each run, Pallas kernels for 0% -> 0%
where the time goes in v1:
time: 155 us
  Pallas kernels  152 us (98%)
  local copies, waits for them, and re-layouts  3.36 us (2%)
    pallas_call x1, Pallas kernels, shards(): pl.pallas_call(kernel, out_shape=jax.ShapeDtypeStruct((64, WIDTH), BF16),...  152 us
    unnamed x2, local copies, waits for them, and re-layouts  3.36 us

profile of v1, /device:TPU:1, one launch (start us, length us, event | category | flops | bytes accessed | tf_op | source)
XLA Modules:
  0.0 155.3 jit_solution(13082290447385288276)
XLA Ops:
  0.0 1.6 %copy.7 = bf16[48,4,384]{2,0,1:T(8,128)(2,1)} copy(bf16[48,4,384]{2,1,0:T(4,128)(2,1)} %param.5) | data formatting | bytes 294912 | tf_op args[1]
  1.6 151.9 %whole.1 = bf16[64,3072]{1,0:T(8,128)(2,1)} custom-call(s32[64]{0:T(128)} %seg_ref.1, bf16[512,3072]{1,0:T(8,128)(2,1)} %bitcast.6, bf16[8,8,8,3072]{3,2,1,0:T(8,128)(2,1)} %bitcast.7, bf16[4,48,384]{2,1,0:T(8,128)(2,1)} %bitcast.9, bf16[48,512]{1,0:T(8,128)(2,1)} %wo_ref.1), custom_call_target="tpu_custom_call" | custom-call | tf_op jit(solution)/shard_map/whole/pallas_call | solution.py:365
  153.5 1.8 %copy.9 = bf16[1,64,3072]{2,1,0:T(8,128)(2,1)} copy(bf16[1,64,3072]{2,1,0:T(8,128)(2,1)} %bitcast.8) | data formatting | bytes 786432

commit v2 on v1

v2 whole, which is shorter than its diff:
```python
import functools
import math

import jax
import jax.numpy as jnp
from jax import lax
from jax.experimental import pallas as pl
from jax.experimental.pallas import tpu as pltpu
from jax.sharding import PartitionSpec as P

HEAD = 128
MESH = pl.DeviceIdType.MESH
NZ = NY = 8
NX = 4
PIECE = 48
QKV = 3 * HEAD
SLAB = 384
PATCHES = 512
WIDTH = 3072
UP = ((-1, 0), (-1, 1), (-2, 0), (-2, 1), (-3, 0), (-3, 1), (-4, 0))
DOWN = ((1, 1), (1, 0), (2, 1), (2, 0), (3, 1), (3, 0), (4, 1))
F32 = jnp.float32
BF16 = jnp.bfloat16


def nt_dot(a, b):
    return lax.dot_general(a, b, (((1,), (1,)), ((), ())), preferred_element_type=F32)


def nn_dot(a, b):
    return lax.dot_general(a, b, (((1,), (0,)), ((), ())), preferred_element_type=F32)


def softmax_rows(scores):
    top = jnp.max(scores, axis=-1, keepdims=True)
    expo = jnp.exp(scores - top)
    return expo * (1.0 / jnp.sum(expo, axis=-1, keepdims=True))


def kernel(
    seg_ref, x_ref, x4_ref, wq_ref, wo_ref, out_ref,
    xs, xt, w, wo, stage, a, acc, qt, qs, ot, b1, b2, ho, p, c, d, e, f, idc, idr,
    gs, gr, ns, nr, xsem, xrec, ts, tr, vs, vr, loc,
):
    st, fs = lax.axis_index("st"), lax.axis_index("fsdp")
    x, core = st // 2, st % 2
    z, y = fs // NY, fs % NY
    scale = 1.0 / math.sqrt(HEAD)
    sent = []

    def dev_y(k):
        return (st, z * NY + (y + k) % NY)

    def dev_z(k):
        return (st, ((z + k) % NZ) * NY + y)

    def dev_x(k):
        return (((x + k) % NX) * 2 + core, fs)

    sibling = (x * 2 + 1 - core, fs)

    def remote(src, dst, ssem, rsem, dev):
        return pltpu.make_async_remote_copy(
            src_ref=src, dst_ref=dst, send_sem=ssem, recv_sem=rsem, device_id=dev, device_id_type=MESH
        )

    def send(*args):
        copy = remote(*args)
        copy.start()
        sent.append(copy)

    barrier = pltpu.get_barrier_semaphore()

    def greet(k, _):
        pl.semaphore_signal(barrier, inc=1, device_id=(st, (fs + k) % 64), device_id_type=MESH)
        return 0

    lax.fori_loop(1, 64, greet, 0)
    for dev in (dev_x(1), dev_x(-1), sibling):
        pl.semaphore_signal(barrier, inc=1, device_id=dev, device_id_type=MESH)

    cols = pl.ds(pl.multiple_of(st * SLAB, SLAB), SLAB)
    locals_ = [
        pltpu.make_async_copy(x4_ref.at[:, :, :, cols], stage, loc.at[0]),
        pltpu.make_async_copy(wo_ref, wo.at[z, y], loc.at[1]),
        pltpu.make_async_copy(wq_ref.at[0], w.at[0, z, y], loc.at[2]),
        pltpu.make_async_copy(wq_ref.at[1], w.at[1, z, y], loc.at[3]),
        pltpu.make_async_copy(x_ref, xs, loc.at[4]),
    ]
    for cp in locals_:
        cp.start()

    sub8 = lax.broadcasted_iota(jnp.int32, (8, HEAD), 0)
    lane = lax.broadcasted_iota(jnp.int32, (8, PATCHES), 1)
    row = jnp.zeros((8, PATCHES), jnp.int32)
    for t in range(64):
        sid = seg_ref[t]
        idc[t * 8 : (t + 1) * 8, :] = sub8 + sid * 8
        row = jnp.where(lane // 8 == t, sid * 8, row)
    idr[...] = row + lane % 8

    for cp in locals_[:4]:
        cp.wait()
    own_tile = pltpu.make_async_copy(stage.at[z, y], a.at[st, z, y], loc.at[5])
    own_tile.start()
    own_tile.wait()
    pl.semaphore_wait(barrier, 66)

    class Stream:
        def __init__(self, number, y_first, flip, view):
            self.n, self.y_first, self.flip, self.view = number, y_first, flip, view
            self.ac, self.bc = (y, z) if y_first else (z, y)
            self.da, self.db = (dev_y, dev_z) if y_first else (dev_z, dev_y)

        def piece(self, at):
            return self.view(self.bc, at) if self.y_first else self.view(at, self.bc)

        def slab(self, bt, sub):
            four = pl.ds(4 * sub, 4)
            return self.view(bt, four) if self.y_first else self.view(four, bt)

        def sems(self, i):
            return gs.at[self.n, i], gr.at[self.n, i]

        def first_own(self):
            right = 1 if not self.flip else -1
            own = self.piece(self.ac)
            send(own, own, *self.sems(0), self.da(right))
            send(own, own, *self.sems(4), self.da(-right))

        def first(self, k):
            right = 1 if not self.flip else -1
            for way, base, last in ((right, 0, 4), (-right, 4, 3)):
                if k <= last:
                    got = self.piece((self.ac - way * k) % 8)
                    remote(got, got, *self.sems(base + k - 1), self.da(-way)).wait_recv()
                    if k < last:
                        send(got, got, *self.sems(base + k), self.da(way))

        def second_own(self):
            for sub in (0, 1):
                for way, base, chain in ((1, 7, UP), (-1, 14, DOWN)):
                    blk = self.slab(self.bc, chain[sub][1])
                    send(blk, blk, *self.sems(base + sub), self.db(way))

        def second(self, i):
            for way, base, chain in ((1, 7, UP), (-1, 14, DOWN)):
                off, sub = chain[i]
                got = self.slab((self.bc + off) % 8, sub)
                remote(got, got, *self.sems(base + i), self.db(-way)).wait_recv()
                if i <= 4:
                    send(got, got, *self.sems(base + i + 2), self.db(way))

    def head_stream(number, kind, h, y_first, flip):
        return Stream(number, y_first, flip, lambda zi, yi: w.at[kind, zi, yi, ..., pl.ds(h * QKV, QKV)])

    t0 = head_stream(0, 1, 0, True, False)
    t1 = head_stream(1, 1, 1, False, True)
    s0 = head_stream(2, 0, 0, True, True)
    s1 = head_stream(3, 0, 1, False, False)
    o0 = Stream(4, True, False, lambda zi, yi: wo.at[zi, yi, ..., pl.ds(0, 32), :])
    o1 = Stream(5, False, True, lambda zi, yi: wo.at[zi, yi, ..., pl.ds(32, 16), :])

    def both(one, two, i):
        one.second(i)
        two.second(i)

    t0.first_own()
    t1.first_own()

    def tile_out(k):
        to = (fs + k) % 64
        return remote(stage.at[to // NY, to % NY], a.at[st, z, y], ns.at[k - 1], nr.at[k - 1], (st, to))

    def tile_in(k):
        to = (fs + 64 - k) % 64
        got = a.at[st, to // NY, to % NY]
        return remote(got, got, ns.at[k - 1], nr.at[k - 1], (st, to))

    def start_tile(k, _):
        tile_out(k).start()
        return 0

    def await_tile(k, _):
        tile_in(k).wait_recv()
        return 0

    def end_tile(k, _):
        tile_out(k).wait_send()
        return 0

    lax.fori_loop(1, 64, start_tile, 0)
    others = (s0, s1, o1, o0)
    for s in others:
        s.first_own()
    for k in range(1, 5):
        t0.first(k)
        t1.first(k)
    t0.second_own()
    t1.second_own()

    def first_others(k):
        for s in others:
            s.first(k)

    def assemble(sl):
        def body(i, _):
            v = a[sl, i].astype(F32).reshape(64, SLAB).astype(BF16)
            rows = pl.ds(pl.multiple_of(i * 64, 64), 64)
            xt[rows, pl.ds(pl.multiple_of(sl * SLAB, SLAB), SLAB)] = v
            return 0

        lax.fori_loop(0, 8, body, 0)

    sl_m, sl_p, sl_2 = (((x + k) % NX) * 2 + core for k in (3, 1, 2))
    lo, hi = pl.ds(0, 4), pl.ds(4, 4)

    def xmove(ref, i, dev):
        return ref, ref, xsem.at[i], xrec.at[i], dev

    def from_sibling(i, sl):
        other = sl + 1 - 2 * core
        remote(*xmove(a.at[other], 4 + i, sibling)).wait_recv()
        assemble(other)

    first_others(1)
    first_others(2)
    both(t0, t1, 0)
    first_others(3)
    lax.fori_loop(1, 64, await_tile, 0)
    send(*xmove(a.at[st], 0, dev_x(1)))
    send(*xmove(a.at[st], 1, dev_x(-1)))
    send(*xmove(a.at[st], 4, sibling))
    both(t0, t1, 1)
    first_others(4)
    assemble(st)
    both(t0, t1, 2)
    remote(*xmove(a.at[sl_m], 0, dev_x(-1))).wait_recv()
    send(*xmove(a.at[sl_m, lo], 2, dev_x(1)))
    send(*xmove(a.at[sl_m], 5, sibling))
    remote(*xmove(a.at[sl_p], 1, dev_x(1))).wait_recv()
    send(*xmove(a.at[sl_p, hi], 3, dev_x(-1)))
    send(*xmove(a.at[sl_p], 6, sibling))
    assemble(sl_m)
    both(t0, t1, 3)
    assemble(sl_p)
    from_sibling(0, st)
    both(t0, t1, 4)
    s0.second_own()
    s1.second_own()
    remote(*xmove(a.at[sl_2, lo], 2, dev_x(-1))).wait_recv()
    remote(*xmove(a.at[sl_2, hi], 3, dev_x(1))).wait_recv()
    send(*xmove(a.at[sl_2], 7, sibling))
    assemble(sl_2)
    from_sibling(1, sl_m)
    both(t0, t1, 5)
    from_sibling(2, sl_p)
    from_sibling(3, sl_2)
    both(t0, t1, 6)

    def proj(rows, kind, i):
        part = nn_dot(rows[:, i * 2 * SLAB : (i + 1) * 2 * SLAB], w[kind, 2 * i : 2 * i + 2].reshape(2 * SLAB, 2 * QKV))
        acc[...] = part if i == 0 else acc[...] + part

    def temporal(h):
        base = h * QKV
        for b, start in enumerate((0, 64, 192, 256)):
            rows, keys = pl.ds(b * 128, 128), pl.ds(start, 256)
            s = nt_dot(qt[rows, base : base + HEAD], qt[keys, base + HEAD : base + 2 * HEAD]) * scale
            same = idc[rows, 0:1] == idr[0:1, keys]
            wt = softmax_rows(jnp.where(same, s, -1e30)).astype(BF16)
            o = nn_dot(wt, qt[keys, base + 2 * HEAD : base + QKV])
            ot[2 * b : 2 * b + 2, :, :, h * HEAD : (h + 1) * HEAD] = o.reshape(2, 8, 8, HEAD).astype(BF16)

    def spatial(h, half):
        base = h * QKV

        def body(i, _):
            rows = pl.ds(pl.multiple_of(i * 128, 128), 128)
            s = nt_dot(qs[rows, base : base + HEAD], qs[:, base + HEAD : base + 2 * HEAD]) * scale
            o = nn_dot(softmax_rows(s).astype(BF16), qs[:, base + 2 * HEAD : base + QKV])
            ho[rows, h * HEAD : (h + 1) * HEAD] = o.astype(BF16)
            return 0

        lax.fori_loop(2 * half, 2 * half + 2, body, 0)

    proj(xt, 1, 0)
    proj(xt, 1, 1)
    both(s0, s1, 0)
    proj(xt, 1, 2)
    proj(xt, 1, 3)
    qt[...] = acc[...].astype(BF16)
    both(s0, s1, 1)
    temporal(0)
    temporal(1)
    for k in range(1, 8):
        send(ot.at[(z + k) % NZ], b1.at[z], ts.at[k - 1], tr.at[k - 1], dev_z(k))
    back = pltpu.make_async_copy(ot.at[z], b1.at[z], loc.at[6])
    back.start()
    both(s0, s1, 2)
    back.wait()
    for k in range(1, 8):
        got = b1.at[(z - k) % NZ]
        remote(got, got, ts.at[k - 1], tr.at[k - 1], dev_z(-k)).wait_recv()
    for k in range(1, 8):
        send(b1.at[:, (y + k) % NY], b2.at[:, y], ts.at[6 + k], tr.at[6 + k], dev_y(k))
    back2 = pltpu.make_async_copy(b1.at[:, y], b2.at[:, y], loc.at[7])
    back2.start()
    both(s0, s1, 3)
    both(s0, s1, 4)
    o1.second_own()
    o0.second_own()
    both(s0, s1, 5)
    back2.wait()
    for k in range(1, 8):
        got = b2.at[:, (y - k) % NY]
        remote(got, got, ts.at[6 + k], tr.at[6 + k], dev_y(-k)).wait_recv()
    for i in range(8):
        ho[i * 64 : (i + 1) * 64, 2 * HEAD :] = b2[i].astype(F32).reshape(64, 2 * HEAD).astype(BF16)
    locals_[4].wait()
    both(s0, s1, 6)
    proj(xs, 0, 0)
    o1.second(0)
    o1.second(1)
    o0.second(0)
    proj(xs, 0, 1)
    proj(xs, 0, 2)
    o1.second(2)
    o0.second(1)
    proj(xs, 0, 3)
    qs[...] = acc[...].astype(BF16)
    o1.second(3)
    spatial(0, 0)
    o1.second(4)
    o0.second(2)
    spatial(0, 1)
    o1.second(5)
    spatial(1, 0)
    o0.second(3)
    spatial(1, 1)
    o1.second(6)

    order = (0, -1, 1, -2, 2, -3, 3, 4)
    xp, xm, x2 = (x + 1) % NX, (x + 3) % NX, (x + 2) % NX
    top, low = pl.ds(0, 32), pl.ds(32, 32)

    def ring(ref_from, ref_to, j, i, dev):
        return ref_from, ref_to, vs.at[j, i], vr.at[j, i], dev

    def project(j):
        n = (z + order[j]) % NZ
        o = nt_dot(ho[...], wo[n].reshape(SLAB, 4 * HEAD))
        p[j] = o.astype(BF16).reshape(NX, 2, 64, SLAB)
        send(*ring(p.at[j, :, 1 - core], c.at[j], j, 0, sibling))

    def pair(j):
        remote(*ring(c.at[j], c.at[j], j, 0, sibling)).wait_recv()
        d[j] = (p[j, :, core].astype(F32) + c[j].astype(F32)).astype(BF16)
        send(*ring(d.at[j, x2, top], e.at[j, 0], j, 1, dev_x(1)))
        send(*ring(d.at[j, x2, low], e.at[j, 1], j, 2, dev_x(-1)))

    def relay(j):
        remote(*ring(e.at[j, 0], e.at[j, 0], j, 1, dev_x(-1))).wait_recv()
        d[j, xp, 0:32] = (d[j, xp, 0:32].astype(F32) + e[j, 0].astype(F32)).astype(BF16)
        send(*ring(d.at[j, xp], f.at[j, 0], j, 3, dev_x(1)))
        remote(*ring(e.at[j, 1], e.at[j, 1], j, 2, dev_x(1))).wait_recv()
        d[j, xm, 32:64] = (d[j, xm, 32:64].astype(F32) + e[j, 1].astype(F32)).astype(BF16)
        send(*ring(d.at[j, xm], f.at[j, 1], j, 4, dev_x(-1)))

    def finish(j):
        remote(*ring(f.at[j, 0], f.at[j, 0], j, 3, dev_x(-1))).wait_recv()
        remote(*ring(f.at[j, 1], f.at[j, 1], j, 4, dev_x(1))).wait_recv()
        total = d[j, x].astype(F32) + f[j, 0].astype(F32) + f[j, 1].astype(F32)
        n = (z + order[j]) % NZ
        out_ref[:, pl.ds(pl.multiple_of(n * SLAB, SLAB), SLAB)] = total.astype(BF16)

    for j in range(11):
        if j == 3:
            o0.second(4)
        if j == 5:
            o0.second(5)
        if j == 7:
            o0.second(6)
        if j < 8:
            project(j)
        if 1 <= j <= 8:
            pair(j - 1)
        if 2 <= j <= 9:
            relay(j - 2)
        if 3 <= j:
            finish(j - 3)
    for copy in sent:
        copy.wait_send()
    lax.fori_loop(1, 64, end_tile, 0)


def shards(normed, qkv_weight, out_weight, segment_ids):
    rows = normed.reshape(PATCHES, WIDTH)
    tiles = normed.reshape(NZ, NY, 8, WIDTH)
    kinds = jnp.transpose(qkv_weight.reshape(PIECE, 2, 2 * QKV), (1, 0, 2))
    dma = pltpu.SemaphoreType.DMA
    out = pl.pallas_call(
        kernel,
        out_shape=jax.ShapeDtypeStruct((64, WIDTH), BF16),
        in_specs=[pl.BlockSpec(memory_space=pltpu.SMEM)] + [pl.BlockSpec(memory_space=pl.ANY)] * 4,
        out_specs=pl.BlockSpec(memory_space=pltpu.VMEM),
        scratch_shapes=[
            pltpu.VMEM((PATCHES, WIDTH), BF16),
            pltpu.VMEM((PATCHES, WIDTH), BF16),
            pltpu.VMEM((2, NZ, NY, PIECE, 2 * QKV), BF16),
            pltpu.VMEM((NZ, NY, PIECE, 4 * HEAD), BF16),
            pltpu.VMEM((NZ, NY, 8, SLAB), BF16),
            pltpu.VMEM((8, NZ, NY, 8, SLAB), BF16),
            pltpu.VMEM((PATCHES, 2 * QKV), F32),
            pltpu.VMEM((PATCHES, 2 * QKV), BF16),
            pltpu.VMEM((PATCHES, 2 * QKV), BF16),
            pltpu.VMEM((NZ, NY, 8, 2 * HEAD), BF16),
            pltpu.VMEM((NZ, NY, 8, 2 * HEAD), BF16),
            pltpu.VMEM((NZ, NY, 8, 2 * HEAD), BF16),
            pltpu.VMEM((PATCHES, 4 * HEAD), BF16),
            pltpu.VMEM((8, NX, 2, 64, SLAB), BF16),
            pltpu.VMEM((8, NX, 64, SLAB), BF16),
            pltpu.VMEM((8, NX, 64, SLAB), BF16),
            pltpu.VMEM((8, 2, 32, SLAB), BF16),
            pltpu.VMEM((8, 2, 64, SLAB), BF16),
            pltpu.VMEM((PATCHES, HEAD), jnp.int32),
            pltpu.VMEM((8, PATCHES), jnp.int32),
            dma((6, 21)), dma((6, 21)),
            dma((63,)), dma((63,)),
            dma((8,)), dma((8,)),
            dma((14,)), dma((14,)),
            dma((8, 5)), dma((8, 5)),
            dma((8,)),
        ],
        compiler_params=pltpu.CompilerParams(
            collective_id=0, has_side_effects=True, vmem_limit_bytes=60 * 2**20
        ),
        name="whole",
    )(segment_ids, rows, tiles, kinds, out_weight)
    return out.reshape(1, 64, WIDTH)


def solution(mesh):
    return jax.shard_map(
        shards,
        mesh=mesh,
        in_specs=(P("fsdp", None, None), P("fsdp", "st", None), P("fsdp", "st"), P()),
        out_specs=P("fsdp", "st", None),
        check_vma=False,
    )
```

time: 155 us -> 148 us (0.955)
  Pallas kernels: 152 us -> 145 us
    pallas_call x1, Pallas kernels: 152 us -> 145 us  [shards(): pl.pallas_call(kernel, out_shape=jax.ShapeDtypeStruct((64, WIDTH), BF16),...]
    reshape x0 -> x2, local copies, waits for them, and re-layouts: none -> 1.68 us  [shards(): kinds = jnp.transpose(qkv_weight.reshape(PIECE, 2, 2 * QKV), (1, 0, 2))]
    unnamed x2 -> x1, local copies, waits for them, and re-layouts: 3.36 us -> 1.77 us
where the time goes in v2:
time: 148 us
  Pallas kernels  145 us (98%)
  local copies, waits for them, and re-layouts  3.45 us (2%)
    pallas_call x1, Pallas kernels, shards(): pl.pallas_call(kernel, out_shape=jax.ShapeDtypeStruct((64, WIDTH), BF16),...  145 us

profile of v2, /device:TPU:1, one launch (start us, length us, event | category | flops | bytes accessed | tf_op | source)
XLA Modules:
  0.0 148.1 jit_solution(8193814029827622949)
XLA Ops:
  0.0 1.0 reshape.14
  1.0 0.7 copy.7
  1.7 144.6 %whole.1 = bf16[64,3072]{1,0:T(8,128)(2,1)} custom-call(s32[64]{0:T(128)} %seg_ref.1, bf16[512,3072]{1,0:T(8,128)(2,1)} %bitcast.6, bf16[8,8,8,3072]{3,2,1,0:T(8,128)(2,1)} %bitcast.7, bf16[2,48,768]{2,1,0:T(8,128)(2,1)} %bitcast.9, bf16[48,512]{1,0:T(8,128)(2,1)} %wo_ref.1), custom_call_target="tpu_custom_call" | custom-call | tf_op jit(solution)/shard_map/whole/pallas_call | solution.py:402
  146.3 1.8 %copy.9 = bf16[1,64,3072]{2,1,0:T(8,128)(2,1)} copy(bf16[1,64,3072]{2,1,0:T(8,128)(2,1)} %bitcast.8) | data formatting | bytes 786432

commit v3 on v2

--- a/solution.py
+++ b/solution.py
@@ -189,19 +189,15 @@
         tile_out(k).wait_send()
         return 0
 
-    lax.fori_loop(1, 64, start_tile, 0)
     others = (s0, s1, o1, o0)
     for s in others:
         s.first_own()
     for k in range(1, 5):
-        t0.first(k)
-        t1.first(k)
+        lax.fori_loop(16 * k - 15, min(16 * k + 1, 64), start_tile, 0)
+        for s in (t0, t1, *others):
+            s.first(k)
     t0.second_own()
     t1.second_own()
-
-    def first_others(k):
-        for s in others:
-            s.first(k)
 
     def assemble(sl):
         def body(i, _):
@@ -223,17 +219,14 @@
         remote(*xmove(a.at[other], 4 + i, sibling)).wait_recv()
         assemble(other)
 
-    first_others(1)
-    first_others(2)
-    both(t0, t1, 0)
-    first_others(3)
     lax.fori_loop(1, 64, await_tile, 0)
     send(*xmove(a.at[st], 0, dev_x(1)))
     send(*xmove(a.at[st], 1, dev_x(-1)))
     send(*xmove(a.at[st], 4, sibling))
+    both(t0, t1, 0)
+    assemble(st)
     both(t0, t1, 1)
-    first_others(4)
-    assemble(st)
+    from_sibling(0, st)
     both(t0, t1, 2)
     remote(*xmove(a.at[sl_m], 0, dev_x(-1))).wait_recv()
     send(*xmove(a.at[sl_m, lo], 2, dev_x(1)))
@@ -244,7 +237,6 @@
     assemble(sl_m)
     both(t0, t1, 3)
     assemble(sl_p)
-    from_sibling(0, st)
     both(t0, t1, 4)
     s0.second_own()
     s1.second_own()
@@ -262,6 +254,20 @@
         part = nn_dot(rows[:, i * 2 * SLAB : (i + 1) * 2 * SLAB], w[kind, 2 * i : 2 * i + 2].reshape(2 * SLAB, 2 * QKV))
         acc[...] = part if i == 0 else acc[...] + part
 
+    def proj_slab(off, first=False):
+        n = (z + off) % NZ
+        part = nn_dot(
+            xs[:, pl.ds(pl.multiple_of(n * SLAB, SLAB), SLAB)], w[0, n, :, :, 0:QKV].reshape(SLAB, QKV)
+        )
+        acc[:, 0:QKV] = part if first else acc[:, 0:QKV] + part
+
+    def proj_second(i):
+        part = nn_dot(
+            xs[:, i * 2 * SLAB : (i + 1) * 2 * SLAB],
+            w[0, 2 * i : 2 * i + 2, :, :, QKV:].reshape(2 * SLAB, QKV),
+        )
+        acc[:, QKV:] = part if i == 0 else acc[:, QKV:] + part
+
     def temporal(h):
         base = h * QKV
         for b, start in enumerate((0, 64, 192, 256)):
@@ -274,15 +280,10 @@
 
     def spatial(h, half):
         base = h * QKV
-
-        def body(i, _):
-            rows = pl.ds(pl.multiple_of(i * 128, 128), 128)
-            s = nt_dot(qs[rows, base : base + HEAD], qs[:, base + HEAD : base + 2 * HEAD]) * scale
-            o = nn_dot(softmax_rows(s).astype(BF16), qs[:, base + 2 * HEAD : base + QKV])
-            ho[rows, h * HEAD : (h + 1) * HEAD] = o.astype(BF16)
-            return 0
-
-        lax.fori_loop(2 * half, 2 * half + 2, body, 0)
+        rows = pl.ds(half * 256, 256)
+        s = nt_dot(qs[rows, base : base + HEAD], qs[:, base + HEAD : base + 2 * HEAD]) * scale
+        o = nn_dot(softmax_rows(s).astype(BF16), qs[:, base + 2 * HEAD : base + QKV])
+        ho[rows, h * HEAD : (h + 1) * HEAD] = o.astype(BF16)
 
     proj(xt, 1, 0)
     proj(xt, 1, 1)
@@ -292,12 +293,15 @@
     qt[...] = acc[...].astype(BF16)
     both(s0, s1, 1)
     temporal(0)
+    both(s0, s1, 2)
     temporal(1)
     for k in range(1, 8):
         send(ot.at[(z + k) % NZ], b1.at[z], ts.at[k - 1], tr.at[k - 1], dev_z(k))
     back = pltpu.make_async_copy(ot.at[z], b1.at[z], loc.at[6])
     back.start()
-    both(s0, s1, 2)
+    locals_[4].wait()
+    both(s0, s1, 3)
+    proj_slab(0, True)
     back.wait()
     for k in range(1, 8):
         got = b1.at[(z - k) % NZ]
@@ -306,39 +310,44 @@
         send(b1.at[:, (y + k) % NY], b2.at[:, y], ts.at[6 + k], tr.at[6 + k], dev_y(k))
     back2 = pltpu.make_async_copy(b1.at[:, y], b2.at[:, y], loc.at[7])
     back2.start()
-    both(s0, s1, 3)
     both(s0, s1, 4)
     o1.second_own()
     o0.second_own()
+    proj_slab(-1)
+    proj_slab(1)
     both(s0, s1, 5)
+    proj_slab(-2)
+    proj_slab(2)
+    o1.second(0)
+    both(s0, s1, 6)
+    o1.second(1)
+    o0.second(0)
+    proj_slab(-3)
+    proj_slab(3)
+    o1.second(2)
+    proj_slab(4)
+    o1.second(3)
+    o0.second(1)
+    proj_second(0)
+    proj_second(1)
+    o1.second(4)
+    proj_second(2)
+    proj_second(3)
+    qs[...] = acc[...].astype(BF16)
+    o1.second(5)
+    o0.second(2)
+    spatial(0, 0)
+    spatial(0, 1)
+    o1.second(6)
     back2.wait()
     for k in range(1, 8):
         got = b2.at[:, (y - k) % NY]
         remote(got, got, ts.at[6 + k], tr.at[6 + k], dev_y(-k)).wait_recv()
     for i in range(8):
         ho[i * 64 : (i + 1) * 64, 2 * HEAD :] = b2[i].astype(F32).reshape(64, 2 * HEAD).astype(BF16)
-    locals_[4].wait()
-    both(s0, s1, 6)
-    proj(xs, 0, 0)
-    o1.second(0)
-    o1.second(1)
-    o0.second(0)
-    proj(xs, 0, 1)
-    proj(xs, 0, 2)
-    o1.second(2)
-    o0.second(1)
-    proj(xs, 0, 3)
-    qs[...] = acc[...].astype(BF16)
-    o1.second(3)
-    spatial(0, 0)
-    o1.second(4)
-    o0.second(2)
-    spatial(0, 1)
-    o1.second(5)
+    o0.second(3)
     spatial(1, 0)
-    o0.second(3)
     spatial(1, 1)
-    o1.second(6)
 
     order = (0, -1, 1, -2, 2, -3, 3, 4)
     xp, xm, x2 = (x + 1) % NX, (x + 3) % NX, (x + 2) % NX
@@ -374,21 +383,17 @@
         n = (z + order[j]) % NZ
         out_ref[:, pl.ds(pl.multiple_of(n * SLAB, SLAB), SLAB)] = total.astype(BF16)
 
-    for j in range(11):
-        if j == 3:
-            o0.second(4)
-        if j == 5:
-            o0.second(5)
-        if j == 7:
-            o0.second(6)
+    for j in range(14):
+        if j in (1, 4, 6):
+            o0.second({1: 4, 4: 5, 6: 6}[j])
         if j < 8:
             project(j)
-        if 1 <= j <= 8:
-            pair(j - 1)
         if 2 <= j <= 9:
-            relay(j - 2)
-        if 3 <= j:
-            finish(j - 3)
+            pair(j - 2)
+        if 4 <= j <= 11:
+            relay(j - 4)
+        if 6 <= j:
+            finish(j - 6)
     for copy in sent:
         copy.wait_send()
     lax.fori_loop(1, 64, end_tile, 0)

time: 148 us -> 137 us (0.926)
  Pallas kernels: 145 us -> 132 us
    pallas_call x1, Pallas kernels: 145 us -> 132 us  [shards(): pl.pallas_call(kernel, out_shape=jax.ShapeDtypeStruct((64, WIDTH), BF16),...]
where the time goes in v3:
time: 137 us; the launch traced here: 136 us
  Pallas kernels  132 us (96%)
  local copies, waits for them, and re-layouts  3.45 us (3%)
    pallas_call x1, Pallas kernels, shards(): pl.pallas_call(kernel, out_shape=jax.ShapeDtypeStruct((64, WIDTH), BF16),...  132 us

profile of v3, /device:TPU:1, one launch (start us, length us, event | category | flops | bytes accessed | tf_op | source)
XLA Modules:
  0.0 135.9 jit_solution(14207413699889689472)
XLA Ops:
  0.0 1.0 reshape.14
  1.0 0.7 copy.7
  1.7 132.4 %whole.1 = bf16[64,3072]{1,0:T(8,128)(2,1)} custom-call(s32[64]{0:T(128)} %seg_ref.1, bf16[512,3072]{1,0:T(8,128)(2,1)} %bitcast.6, bf16[8,8,8,3072]{3,2,1,0:T(8,128)(2,1)} %bitcast.7, bf16[2,48,768]{2,1,0:T(8,128)(2,1)} %bitcast.9, bf16[48,512]{1,0:T(8,128)(2,1)} %wo_ref.1), custom_call_target="tpu_custom_call" | custom-call | tf_op jit(solution)/shard_map/whole/pallas_call | solution.py:407
  134.1 1.8 %copy.9 = bf16[1,64,3072]{2,1,0:T(8,128)(2,1)} copy(bf16[1,64,3072]{2,1,0:T(8,128)(2,1)} %bitcast.8) | data formatting | bytes 786432

commit v4 on v3

--- a/solution.py
+++ b/solution.py
@@ -19,6 +19,7 @@
 WIDTH = 3072
 UP = ((-1, 0), (-1, 1), (-2, 0), (-2, 1), (-3, 0), (-3, 1), (-4, 0))
 DOWN = ((1, 1), (1, 0), (2, 1), (2, 0), (3, 1), (3, 0), (4, 1))
+SPREAD = (1, 7, 2, 6, 3, 5, 4)
 F32 = jnp.float32
 BF16 = jnp.bfloat16
 
@@ -39,7 +40,7 @@
 
 def kernel(
     seg_ref, x_ref, x4_ref, wq_ref, wo_ref, out_ref,
-    xs, xt, w, wo, stage, a, acc, qt, qs, ot, b1, b2, ho, p, c, d, e, f, idc, idr,
+    xs, xt, w, wo, stage, a, acc, qt, qs, ot, b1, b2, ho, p, c, d, e, f, idc, idr, raw,
     gs, gr, ns, nr, xsem, xrec, ts, tr, vs, vr, loc,
 ):
     st, fs = lax.axis_index("st"), lax.axis_index("fsdp")
@@ -83,8 +84,7 @@
     locals_ = [
         pltpu.make_async_copy(x4_ref.at[:, :, :, cols], stage, loc.at[0]),
         pltpu.make_async_copy(wo_ref, wo.at[z, y], loc.at[1]),
-        pltpu.make_async_copy(wq_ref.at[0], w.at[0, z, y], loc.at[2]),
-        pltpu.make_async_copy(wq_ref.at[1], w.at[1, z, y], loc.at[3]),
+        pltpu.make_async_copy(wq_ref, raw, loc.at[2]),
         pltpu.make_async_copy(x_ref, xs, loc.at[4]),
     ]
     for cp in locals_:
@@ -99,8 +99,10 @@
         row = jnp.where(lane // 8 == t, sid * 8, row)
     idr[...] = row + lane % 8
 
-    for cp in locals_[:4]:
+    for cp in locals_[:3]:
         cp.wait()
+    for h in range(4):
+        w[h // 2, z, y, :, h % 2 * QKV : (h % 2 + 1) * QKV] = raw[:, h, :]
     own_tile = pltpu.make_async_copy(stage.at[z, y], a.at[st, z, y], loc.at[5])
     own_tile.start()
     own_tile.wait()
@@ -169,11 +171,11 @@
     t1.first_own()
 
     def tile_out(k):
-        to = (fs + k) % 64
+        to = (fs + 27 * k) % 64
         return remote(stage.at[to // NY, to % NY], a.at[st, z, y], ns.at[k - 1], nr.at[k - 1], (st, to))
 
     def tile_in(k):
-        to = (fs + 64 - k) % 64
+        to = (fs + 37 * k) % 64
         got = a.at[st, to // NY, to % NY]
         return remote(got, got, ns.at[k - 1], nr.at[k - 1], (st, to))
 
@@ -194,10 +196,17 @@
         s.first_own()
     for k in range(1, 5):
         lax.fori_loop(16 * k - 15, min(16 * k + 1, 64), start_tile, 0)
-        for s in (t0, t1, *others):
-            s.first(k)
+        t0.first(k)
+        t1.first(k)
     t0.second_own()
     t1.second_own()
+
+    def first_others(k):
+        for s in others:
+            s.first(k)
+
+    first_others(1)
+    first_others(2)
 
     def assemble(sl):
         def body(i, _):
@@ -224,8 +233,10 @@
     send(*xmove(a.at[st], 1, dev_x(-1)))
     send(*xmove(a.at[st], 4, sibling))
     both(t0, t1, 0)
+    first_others(3)
     assemble(st)
     both(t0, t1, 1)
+    first_others(4)
     from_sibling(0, st)
     both(t0, t1, 2)
     remote(*xmove(a.at[sl_m], 0, dev_x(-1))).wait_recv()
@@ -286,30 +297,30 @@
         ho[rows, h * HEAD : (h + 1) * HEAD] = o.astype(BF16)
 
     proj(xt, 1, 0)
+    both(s0, s1, 0)
     proj(xt, 1, 1)
-    both(s0, s1, 0)
     proj(xt, 1, 2)
     proj(xt, 1, 3)
     qt[...] = acc[...].astype(BF16)
     both(s0, s1, 1)
     temporal(0)
-    both(s0, s1, 2)
     temporal(1)
-    for k in range(1, 8):
+    for k in SPREAD:
         send(ot.at[(z + k) % NZ], b1.at[z], ts.at[k - 1], tr.at[k - 1], dev_z(k))
     back = pltpu.make_async_copy(ot.at[z], b1.at[z], loc.at[6])
     back.start()
-    locals_[4].wait()
-    both(s0, s1, 3)
+    locals_[3].wait()
+    both(s0, s1, 2)
     proj_slab(0, True)
     back.wait()
     for k in range(1, 8):
         got = b1.at[(z - k) % NZ]
         remote(got, got, ts.at[k - 1], tr.at[k - 1], dev_z(-k)).wait_recv()
-    for k in range(1, 8):
+    for k in SPREAD:
         send(b1.at[:, (y + k) % NY], b2.at[:, y], ts.at[6 + k], tr.at[6 + k], dev_y(k))
     back2 = pltpu.make_async_copy(b1.at[:, y], b2.at[:, y], loc.at[7])
     back2.start()
+    both(s0, s1, 3)
     both(s0, s1, 4)
     o1.second_own()
     o0.second_own()
@@ -321,33 +332,32 @@
     o1.second(0)
     both(s0, s1, 6)
     o1.second(1)
-    o0.second(0)
     proj_slab(-3)
     proj_slab(3)
+    proj_slab(4)
     o1.second(2)
-    proj_slab(4)
-    o1.second(3)
-    o0.second(1)
+    o0.second(0)
     proj_second(0)
     proj_second(1)
-    o1.second(4)
+    o1.second(3)
     proj_second(2)
     proj_second(3)
     qs[...] = acc[...].astype(BF16)
-    o1.second(5)
-    o0.second(2)
+    o1.second(4)
+    o0.second(1)
     spatial(0, 0)
     spatial(0, 1)
-    o1.second(6)
+    o1.second(5)
+    spatial(1, 0)
+    spatial(1, 1)
     back2.wait()
     for k in range(1, 8):
         got = b2.at[:, (y - k) % NY]
         remote(got, got, ts.at[6 + k], tr.at[6 + k], dev_y(-k)).wait_recv()
     for i in range(8):
         ho[i * 64 : (i + 1) * 64, 2 * HEAD :] = b2[i].astype(F32).reshape(64, 2 * HEAD).astype(BF16)
-    o0.second(3)
-    spatial(1, 0)
-    spatial(1, 1)
+    o0.second(2)
+    o1.second(6)
 
     order = (0, -1, 1, -2, 2, -3, 3, 4)
     xp, xm, x2 = (x + 1) % NX, (x + 3) % NX, (x + 2) % NX
@@ -383,17 +393,19 @@
         n = (z + order[j]) % NZ
         out_ref[:, pl.ds(pl.multiple_of(n * SLAB, SLAB), SLAB)] = total.astype(BF16)
 
-    for j in range(14):
-        if j in (1, 4, 6):
-            o0.second({1: 4, 4: 5, 6: 6}[j])
-        if j < 8:
-            project(j)
-        if 2 <= j <= 9:
-            pair(j - 2)
-        if 4 <= j <= 11:
-            relay(j - 4)
-        if 6 <= j:
-            finish(j - 6)
+    def run(steps):
+        for stage, j in steps:
+            (project, pair, relay, finish)[stage](j)
+
+    run(((0, 0), (0, 1), (0, 2), (1, 0), (1, 1)))
+    o0.second(3)
+    run(((0, 3), (0, 4), (1, 2), (2, 0), (2, 1), (1, 3), (1, 4)))
+    o0.second(4)
+    run(((2, 2), (2, 3), (3, 0), (3, 1)))
+    o0.second(5)
+    run(((0, 5), (0, 6), (2, 4), (3, 2), (1, 5), (1, 6)))
+    o0.second(6)
+    run(((0, 7), (3, 3), (2, 5), (2, 6), (1, 7), (3, 4), (3, 5), (3, 6), (2, 7), (3, 7)))
     for copy in sent:
         copy.wait_send()
     lax.fori_loop(1, 64, end_tile, 0)
@@ -402,7 +414,6 @@
 def shards(normed, qkv_weight, out_weight, segment_ids):
     rows = normed.reshape(PATCHES, WIDTH)
     tiles = normed.reshape(NZ, NY, 8, WIDTH)
-    kinds = jnp.transpose(qkv_weight.reshape(PIECE, 2, 2 * QKV), (1, 0, 2))
     dma = pltpu.SemaphoreType.DMA
     out = pl.pallas_call(
         kernel,
@@ -430,6 +441,7 @@
             pltpu.VMEM((8, 2, 64, SLAB), BF16),
             pltpu.VMEM((PATCHES, HEAD), jnp.int32),
             pltpu.VMEM((8, PATCHES), jnp.int32),
+            pltpu.VMEM((PIECE, 4, QKV), BF16),
             dma((6, 21)), dma((6, 21)),
             dma((63,)), dma((63,)),
             dma((8,)), dma((8,)),
@@ -441,7 +453,7 @@
             collective_id=0, has_side_effects=True, vmem_limit_bytes=60 * 2**20
         ),
         name="whole",
-    )(segment_ids, rows, tiles, kinds, out_weight)
+    )(segment_ids, rows, tiles, qkv_weight, out_weight)
     return out.reshape(1, 64, WIDTH)
 
 

time: 137 us -> 137 us (level)
  Pallas kernels: 132 us -> 135 us
  local copies, waits for them, and re-layouts: 3.45 us -> 1.77 us
    pallas_call x1, Pallas kernels: 132 us -> 135 us  [shards(): pl.pallas_call(kernel, out_shape=jax.ShapeDtypeStruct((64, WIDTH), BF16),...]
    reshape x2 -> x0, local copies, waits for them, and re-layouts: 1.68 us -> none  [shards(): kinds = jnp.transpose(qkv_weight.reshape(PIECE, 2, 2 * QKV), (1, 0, 2))]
where the time goes in v4:
time: 137 us; the launch traced here: 136 us
  Pallas kernels  135 us (99%)
  local copies, waits for them, and re-layouts  1.77 us (1%)
    pallas_call x1, Pallas kernels, shards(): pl.pallas_call(kernel, out_shape=jax.ShapeDtypeStruct((64, WIDTH), BF16),...  135 us

profile of v4, /device:TPU:1, one launch (start us, length us, event | category | flops | bytes accessed | tf_op | source)
XLA Modules:
  0.0 136.4 jit_solution(8958214885792936038)
XLA Ops:
  0.0 134.6 %whole.1 = bf16[64,3072]{1,0:T(8,128)(2,1)} custom-call(s32[64]{0:T(128)} %seg_ref.1, bf16[512,3072]{1,0:T(8,128)(2,1)} %bitcast.3, bf16[8,8,8,3072]{3,2,1,0:T(8,128)(2,1)} %bitcast.4, bf16[48,4,384]{2,1,0:T(4,128)(2,1)} %wq_ref.1, bf16[48,512]{1,0:T(8,128)(2,1)} %wo_ref.1), custom_call_target="tpu_custom_call" | custom-call | tf_op jit(solution)/shard_map/whole/pallas_call | solution.py:418
  134.6 1.8 %copy.6 = bf16[1,64,3072]{2,1,0:T(8,128)(2,1)} copy(bf16[1,64,3072]{2,1,0:T(8,128)(2,1)} %bitcast.5) | data formatting | bytes 786432

commit v5 on v3

--- a/solution.py
+++ b/solution.py
@@ -19,6 +19,7 @@
 WIDTH = 3072
 UP = ((-1, 0), (-1, 1), (-2, 0), (-2, 1), (-3, 0), (-3, 1), (-4, 0))
 DOWN = ((1, 1), (1, 0), (2, 1), (2, 0), (3, 1), (3, 0), (4, 1))
+SPREAD = (1, 7, 2, 6, 3, 5, 4)
 F32 = jnp.float32
 BF16 = jnp.bfloat16
 
@@ -39,7 +40,7 @@
 
 def kernel(
     seg_ref, x_ref, x4_ref, wq_ref, wo_ref, out_ref,
-    xs, xt, w, wo, stage, a, acc, qt, qs, ot, b1, b2, ho, p, c, d, e, f, idc, idr,
+    xs, xt, w, wo, stage, a, acc, qt, qs, ot, b1, b2, ho, p, c, d, e, f, idc, idr, raw,
     gs, gr, ns, nr, xsem, xrec, ts, tr, vs, vr, loc,
 ):
     st, fs = lax.axis_index("st"), lax.axis_index("fsdp")
@@ -83,8 +84,7 @@
     locals_ = [
         pltpu.make_async_copy(x4_ref.at[:, :, :, cols], stage, loc.at[0]),
         pltpu.make_async_copy(wo_ref, wo.at[z, y], loc.at[1]),
-        pltpu.make_async_copy(wq_ref.at[0], w.at[0, z, y], loc.at[2]),
-        pltpu.make_async_copy(wq_ref.at[1], w.at[1, z, y], loc.at[3]),
+        pltpu.make_async_copy(wq_ref, raw, loc.at[2]),
         pltpu.make_async_copy(x_ref, xs, loc.at[4]),
     ]
     for cp in locals_:
@@ -99,8 +99,10 @@
         row = jnp.where(lane // 8 == t, sid * 8, row)
     idr[...] = row + lane % 8
 
-    for cp in locals_[:4]:
+    for cp in locals_[:3]:
         cp.wait()
+    for h in range(4):
+        w[h // 2, z, y, :, h % 2 * QKV : (h % 2 + 1) * QKV] = raw[:, h, :]
     own_tile = pltpu.make_async_copy(stage.at[z, y], a.at[st, z, y], loc.at[5])
     own_tile.start()
     own_tile.wait()
@@ -169,11 +171,11 @@
     t1.first_own()
 
     def tile_out(k):
-        to = (fs + k) % 64
+        to = (fs + 27 * k) % 64
         return remote(stage.at[to // NY, to % NY], a.at[st, z, y], ns.at[k - 1], nr.at[k - 1], (st, to))
 
     def tile_in(k):
-        to = (fs + 64 - k) % 64
+        to = (fs + 37 * k) % 64
         got = a.at[st, to // NY, to % NY]
         return remote(got, got, ns.at[k - 1], nr.at[k - 1], (st, to))
 
@@ -194,10 +196,17 @@
         s.first_own()
     for k in range(1, 5):
         lax.fori_loop(16 * k - 15, min(16 * k + 1, 64), start_tile, 0)
-        for s in (t0, t1, *others):
-            s.first(k)
+        t0.first(k)
+        t1.first(k)
     t0.second_own()
     t1.second_own()
+
+    def first_others(k):
+        for s in others:
+            s.first(k)
+
+    first_others(1)
+    first_others(2)
 
     def assemble(sl):
         def body(i, _):
@@ -224,8 +233,10 @@
     send(*xmove(a.at[st], 1, dev_x(-1)))
     send(*xmove(a.at[st], 4, sibling))
     both(t0, t1, 0)
+    first_others(3)
     assemble(st)
     both(t0, t1, 1)
+    first_others(4)
     from_sibling(0, st)
     both(t0, t1, 2)
     remote(*xmove(a.at[sl_m], 0, dev_x(-1))).wait_recv()
@@ -286,30 +297,30 @@
         ho[rows, h * HEAD : (h + 1) * HEAD] = o.astype(BF16)
 
     proj(xt, 1, 0)
+    both(s0, s1, 0)
     proj(xt, 1, 1)
-    both(s0, s1, 0)
     proj(xt, 1, 2)
     proj(xt, 1, 3)
     qt[...] = acc[...].astype(BF16)
     both(s0, s1, 1)
     temporal(0)
-    both(s0, s1, 2)
     temporal(1)
-    for k in range(1, 8):
+    for k in SPREAD:
         send(ot.at[(z + k) % NZ], b1.at[z], ts.at[k - 1], tr.at[k - 1], dev_z(k))
     back = pltpu.make_async_copy(ot.at[z], b1.at[z], loc.at[6])
     back.start()
-    locals_[4].wait()
-    both(s0, s1, 3)
+    locals_[3].wait()
+    both(s0, s1, 2)
     proj_slab(0, True)
     back.wait()
     for k in range(1, 8):
         got = b1.at[(z - k) % NZ]
         remote(got, got, ts.at[k - 1], tr.at[k - 1], dev_z(-k)).wait_recv()
-    for k in range(1, 8):
+    for k in SPREAD:
         send(b1.at[:, (y + k) % NY], b2.at[:, y], ts.at[6 + k], tr.at[6 + k], dev_y(k))
     back2 = pltpu.make_async_copy(b1.at[:, y], b2.at[:, y], loc.at[7])
     back2.start()
+    both(s0, s1, 3)
     both(s0, s1, 4)
     o1.second_own()
     o0.second_own()
@@ -402,7 +413,6 @@
 def shards(normed, qkv_weight, out_weight, segment_ids):
     rows = normed.reshape(PATCHES, WIDTH)
     tiles = normed.reshape(NZ, NY, 8, WIDTH)
-    kinds = jnp.transpose(qkv_weight.reshape(PIECE, 2, 2 * QKV), (1, 0, 2))
     dma = pltpu.SemaphoreType.DMA
     out = pl.pallas_call(
         kernel,
@@ -430,6 +440,7 @@
             pltpu.VMEM((8, 2, 64, SLAB), BF16),
             pltpu.VMEM((PATCHES, HEAD), jnp.int32),
             pltpu.VMEM((8, PATCHES), jnp.int32),
+            pltpu.VMEM((PIECE, 4, QKV), BF16),
             dma((6, 21)), dma((6, 21)),
             dma((63,)), dma((63,)),
             dma((8,)), dma((8,)),
@@ -441,7 +452,7 @@
             collective_id=0, has_side_effects=True, vmem_limit_bytes=60 * 2**20
         ),
         name="whole",
-    )(segment_ids, rows, tiles, kinds, out_weight)
+    )(segment_ids, rows, tiles, qkv_weight, out_weight)
     return out.reshape(1, 64, WIDTH)
 
 

time: 137 us -> 135 us (0.985)
  local copies, waits for them, and re-layouts: 3.45 us -> 1.77 us
    reshape x2 -> x0, local copies, waits for them, and re-layouts: 1.68 us -> none  [shards(): kinds = jnp.transpose(qkv_weight.reshape(PIECE, 2, 2 * QKV), (1, 0, 2))]
where the time goes in v5:
time: 135 us; the launch traced here: 134 us
  Pallas kernels  132 us (98%)
  local copies, waits for them, and re-layouts  1.77 us (1%)
    pallas_call x1, Pallas kernels, shards(): pl.pallas_call(kernel, out_shape=jax.ShapeDtypeStruct((64, WIDTH), BF16),...  132 us

profile of v5, /device:TPU:1, one launch (start us, length us, event | category | flops | bytes accessed | tf_op | source)
XLA Modules:
  0.0 134.0 jit_solution(9992483173345716290)
XLA Ops:
  0.0 132.2 %whole.1 = bf16[64,3072]{1,0:T(8,128)(2,1)} custom-call(s32[64]{0:T(128)} %seg_ref.1, bf16[512,3072]{1,0:T(8,128)(2,1)} %bitcast.3, bf16[8,8,8,3072]{3,2,1,0:T(8,128)(2,1)} %bitcast.4, bf16[48,4,384]{2,1,0:T(4,128)(2,1)} %wq_ref.1, bf16[48,512]{1,0:T(8,128)(2,1)} %wo_ref.1), custom_call_target="tpu_custom_call" | custom-call | tf_op jit(solution)/shard_map/whole/pallas_call | solution.py:417
  132.2 1.8 %copy.6 = bf16[1,64,3072]{2,1,0:T(8,128)(2,1)} copy(bf16[1,64,3072]{2,1,0:T(8,128)(2,1)} %bitcast.5) | data formatting | bytes 786432
